TPU v7x, 128 devices: a whole 4x4x4 slice. The times are simulated.
128 devices in a mesh: dp: 16 (over y_hi, x, core), row: 4 (over z), col: 2 (over y_lo).
Axes of the slice: x: 4, y: 4 (y_hi: 2, y_lo: 2; y = y_hi * 2 + y_lo), z: 4, core: 2. Of those that a mesh axis runs over, the one named last changes fastest.
Arguments:
- x_in: bfloat16 [8192, 1024], P('dp', 'row'), may hold values from -24 to 24
- segments: int32 [16, 512], P('dp'), may hold values from 0 to 3, never falling along the last dimension, each value on 1 to 256 neighbouring positions
- expert_ids: int32 [8192, 8], P('dp'), may hold values from 0 to 31, all different within a row; in each aligned block of 512 rows (0 to 511, 512 to 1023, ...) at most 160 rows name the same one
- cotangent: bfloat16 [8192, 1024], P('dp', 'row'), may hold values from -6 to 6
- norm_gain1: float32 [1024], P('row'), may hold values from 0.5 to 1.5
- w_query: bfloat16 [1024, 1024], P('row', 'col'), may hold values from -12 to 12
- w_key: bfloat16 [1024, 512], P('row', 'col'), may hold values from -1 to 1
- w_value: bfloat16 [1024, 512], P('row', 'col'), may hold values from -0.1875 to 0.1875
- w_out: bfloat16 [1024, 1024], P('col', 'row'), may hold values from -1.5 to 1.5
- norm_gain2: float32 [1024], P('row'), may hold values from 0.5 to 1.5
- w_router: bfloat16 [1024, 32], P('row'), may hold values from -24 to 24
- w_gate: bfloat16 [32, 1024, 512], P(None, 'row', 'col'), may hold values from -0.1875 to 0.1875
- w_up: bfloat16 [32, 1024, 512], P(None, 'row', 'col'), may hold values from -0.1875 to 0.1875
- w_down: bfloat16 [32, 512, 1024], P(None, 'col', 'row'), may hold values from -0.25 to 0.25
Outputs:
- block_out: bfloat16 [8192, 1024], P('dp', 'row')
- grad_input: bfloat16 [8192, 1024], P('dp', 'row')
- grad_query: float32 [1024, 1024], P('row', 'col')
- grad_key: float32 [1024, 512], P('row', 'col')
- grad_value: float32 [1024, 512], P('row', 'col')
- grad_out: float32 [1024, 1024], P('col', 'row')
- grad_router: float32 [1024, 32], P('row')
- grad_gate: float32 [32, 1024, 512], P('dp', 'row', 'col')
- grad_up: float32 [32, 1024, 512], P('dp', 'row', 'col')
- grad_down: float32 [32, 512, 1024], P('dp', 'col', 'row')
- grad_gain1: float32 [1024], P('row')
- grad_gain2: float32 [1024], P('row')
Inputs may be any that keep to these rules, and one draw needn't show every extreme that they name: `expert_ids`: each token names 8 different experts; within one sequence no expert is named by more than 160 tokens, and in some sequence one is named by exactly 160. `segments`: segment numbers never fall along a sequence; a segment holds at most 256 tokens, and some segment holds exactly that many.
All inputs are finite; a program needn't handle non-finite values.
Results may differ from a plain program's by a relative error of at most 0.0117.
The roundings to bfloat16 on the way count: a program that leaves them out, or rounds other values in their place, can miss the bound.
Values may be sent and summed in bfloat16 or wider, within the bound.
A program may use at most 192 MiB of HBM per device.

v0:
```python
import jax
import jax.numpy as jnp
from jax import lax
from jax.sharding import PartitionSpec as P

D = 1024
HEAD_DIM = 64
EXPERTS = 32
TOPK = 8
CAP = 160
EPSILON = 1e-06
ROPE_BASE = 10000.0
MASKED = -1e30


def rope_tables(positions):
    half_dim = HEAD_DIM // 2
    exponent = jnp.arange(half_dim).astype(jnp.float32) * (2.0 / HEAD_DIM)
    angles = positions.astype(jnp.float32)[:, None] * (ROPE_BASE ** (-exponent))[None, :]
    return (jnp.cos(angles)[:, None, :], jnp.sin(angles)[:, None, :])


def rotate(values_in, cosine, sine_part):
    half_dim = values_in.shape[-1] // 2
    low_half = values_in[..., :half_dim]
    high_half = values_in[..., half_dim:]
    return jnp.concatenate(
        [low_half * cosine - high_half * sine_part, high_half * cosine + low_half * sine_part],
        axis=-1,
    )


def slot_tables(route_rows):
    count_pairs = route_rows.shape[0] * route_rows.shape[1]
    flat_routes = route_rows.reshape(-1)
    expert_hits = (flat_routes[:, None] == jnp.arange(EXPERTS, dtype=jnp.int32)[None, :]).astype(
        jnp.int32
    )
    running = jnp.cumsum(expert_hits, axis=0)
    before = jnp.sum((running - 1) * expert_hits, axis=1)
    slot_of = flat_routes * CAP + before
    pair_of = (
        jnp.full((EXPERTS * CAP,), count_pairs, jnp.int32)
        .at[slot_of]
        .set(jnp.arange(count_pairs, dtype=jnp.int32))
    )
    return (slot_of, pair_of)


def row_total(vector):
    return lax.psum(vector, "row")


def col_total(matrix):
    return lax.psum(matrix, "col")


def head_share(matrix):
    return lax.psum_scatter(matrix, "row", scatter_dimension=0, tiled=True)


def head_collect(matrix):
    return lax.all_gather(matrix, "row", axis=0, tiled=True)


def slot_share(matrix):
    return lax.psum_scatter(matrix, "row", scatter_dimension=0, tiled=True)


def slot_collect(matrix):
    return lax.all_gather(matrix, "row", axis=0, tiled=True)


def norm_inverse(residual):
    squares = row_total(jnp.sum(residual * residual, axis=1))
    return lax.rsqrt(squares / D + EPSILON)[:, None]


def norm_backward(residual, inverse, gain, grad_normed):
    weighted = grad_normed * gain
    project = (row_total(jnp.sum(weighted * residual, axis=1)) / D)[:, None]
    grad_residual = inverse * weighted - residual * inverse**3 * project
    grad_gain = jnp.sum(grad_normed * residual * inverse, axis=0)
    return (grad_residual, grad_gain)


def on_device(
    x_in,
    segments,
    expert_ids,
    cotangent,
    norm_gain1,
    w_query,
    w_key,
    w_value,
    w_out,
    norm_gain2,
    w_router,
    w_gate,
    w_up,
    w_down,
):
    f32 = jnp.float32
    low = jnp.bfloat16
    length = x_in.shape[0]
    feature_part = x_in.shape[1]
    quarters = lax.axis_size("row")
    own_rows = length // quarters
    own_start = lax.axis_index("row") * own_rows
    query_width = w_query.shape[1]
    key_width = w_key.shape[1]
    heads_here = query_width // HEAD_DIM
    key_heads = key_width // HEAD_DIM
    group_size = heads_here // key_heads
    score_scale = HEAD_DIM ** (-0.5)
    residual = x_in.astype(f32)
    scale_attn = norm_inverse(residual)
    normed_attn = (residual * scale_attn * norm_gain1).astype(low)
    joined_proj = jnp.concatenate([w_query, w_key, w_value], axis=1)
    projected = head_share(jnp.dot(normed_attn, joined_proj, preferred_element_type=f32))
    positions = own_start + jnp.arange(own_rows, dtype=jnp.int32)
    cosine, sine_part = rope_tables(positions)
    queries = rotate(
        projected[:, :query_width].reshape(own_rows, heads_here, HEAD_DIM), cosine, sine_part
    ).astype(low)
    own_keys = rotate(
        projected[:, query_width : query_width + key_width].reshape(own_rows, key_heads, HEAD_DIM),
        cosine,
        sine_part,
    ).astype(low)
    own_values = projected[:, query_width + key_width :].astype(low)
    key_value = head_collect(
        jnp.concatenate([own_keys.reshape(own_rows, key_width), own_values], axis=1)
    )
    keys_wide = jnp.repeat(
        key_value[:, :key_width].reshape(length, key_heads, HEAD_DIM), group_size, axis=1
    )
    values_wide = jnp.repeat(
        key_value[:, key_width:].reshape(length, key_heads, HEAD_DIM), group_size, axis=1
    )
    segment_all = segments.reshape(-1)
    key_places = jnp.arange(length, dtype=jnp.int32)
    block_rows = min(256, own_rows)
    blocks = own_rows // block_rows
    query_blocks = queries.reshape(blocks, block_rows, heads_here, HEAD_DIM)
    place_blocks = positions.reshape(blocks, block_rows)
    segment_blocks = lax.dynamic_slice_in_dim(segment_all, own_start, own_rows).reshape(
        blocks, block_rows
    )

    def block_scores(query_block, place_block, segment_block):
        scores = (
            jnp.einsum("qhd,khd->hqk", query_block, keys_wide, preferred_element_type=f32)
            * score_scale
        )
        allowed = (key_places[None, :] <= place_block[:, None]) & (
            segment_all[None, :] == segment_block[:, None]
        )
        return jnp.where(allowed[None], scores, MASKED)

    def forward_block(unused_carry, inputs):
        query_block, place_block, segment_block = inputs
        scores = block_scores(query_block, place_block, segment_block)
        top_score = jnp.max(scores, axis=2, keepdims=True)
        log_total = top_score + jnp.log(jnp.sum(jnp.exp(scores - top_score), axis=2, keepdims=True))
        weights_low = jnp.exp(scores - log_total).astype(low)
        attended = jnp.einsum(
            "hqk,khd->qhd", weights_low, values_wide, preferred_element_type=f32
        ).astype(low)
        return (unused_carry, (attended, log_total))

    _, (attended_blocks, total_blocks) = lax.scan(
        forward_block, jnp.zeros((), jnp.int32), (query_blocks, place_blocks, segment_blocks)
    )
    attended_all = head_collect(attended_blocks.reshape(own_rows, query_width))
    resid_mid = residual + col_total(jnp.dot(attended_all, w_out, preferred_element_type=f32))
    scale_ffn = norm_inverse(resid_mid)
    normed_ffn = (resid_mid * scale_ffn * norm_gain2).astype(low)
    logits = lax.psum(jnp.dot(normed_ffn, w_router, preferred_element_type=f32), "row")
    gate_probs = jax.nn.softmax(jnp.take_along_axis(logits, expert_ids, axis=1), axis=1)
    slot_of, pair_of = slot_tables(expert_ids)
    owner_row = pair_of // TOPK
    padded = jnp.concatenate([normed_ffn, jnp.zeros((1, feature_part), low)], axis=0)
    dispatched = jnp.take(padded, owner_row, axis=0).reshape(EXPERTS, CAP, feature_part)
    both_weights = jnp.concatenate([w_gate, w_up], axis=2)
    hidden_width = w_gate.shape[2]
    pre_act = jnp.einsum("ecd,edf->ecf", dispatched, both_weights, preferred_element_type=f32)
    pre_own = slot_share(pre_act.reshape(EXPERTS * CAP, 2 * hidden_width))
    gate_act = pre_own[:, :hidden_width]
    up_act = pre_own[:, hidden_width:]
    sigmoid_gate = jax.nn.sigmoid(gate_act)
    hidden_own = (gate_act * sigmoid_gate * up_act).astype(low)
    hidden_all = slot_collect(hidden_own).reshape(EXPERTS, CAP, hidden_width)
    expert_out = jnp.einsum("ecf,efd->ecd", hidden_all, w_down, preferred_element_type=f32).reshape(
        EXPERTS * CAP, feature_part
    )
    picked = jnp.take(expert_out, slot_of, axis=0).reshape(length, TOPK, feature_part)
    resid_out = resid_mid + col_total(jnp.sum(gate_probs[:, :, None] * picked, axis=1))
    block_out = resid_out.astype(low)
    grad_top = cotangent.astype(f32)
    grad_prob = lax.psum(jnp.sum(grad_top[:, None, :] * picked, axis=2), ("row", "col"))
    grad_chosen = gate_probs * (grad_prob - jnp.sum(gate_probs * grad_prob, axis=1, keepdims=True))
    expert_hits = (
        expert_ids[:, :, None] == jnp.arange(EXPERTS, dtype=jnp.int32)[None, None, :]
    ).astype(f32)
    grad_logits = jnp.sum(expert_hits * grad_chosen[:, :, None], axis=1).astype(low)
    grad_router = jnp.dot(normed_ffn.T, grad_logits, preferred_element_type=f32)
    spread = (gate_probs[:, :, None] * grad_top[:, None, :]).reshape(length * TOPK, feature_part)
    spread = jnp.concatenate([spread, jnp.zeros((1, feature_part), f32)], axis=0)
    slot_grad = jnp.take(spread, pair_of, axis=0).astype(low).reshape(EXPERTS, CAP, feature_part)
    hidden_grad = slot_share(
        jnp.einsum("ecd,efd->ecf", slot_grad, w_down, preferred_element_type=f32).reshape(
            EXPERTS * CAP, hidden_width
        )
    )
    grad_pre = jnp.concatenate(
        [
            hidden_grad * up_act * sigmoid_gate * (1.0 + gate_act * (1.0 - sigmoid_gate)),
            hidden_grad * gate_act * sigmoid_gate,
        ],
        axis=1,
    ).astype(low)
    grad_pre_all = slot_collect(grad_pre).reshape(EXPERTS, CAP, 2 * hidden_width)
    slot_input = jnp.einsum(
        "ecf,edf->ecd", grad_pre_all, both_weights, preferred_element_type=f32
    ).reshape(EXPERTS * CAP, feature_part)
    grad_both_full = jnp.einsum(
        "ecd,ecf->edf", dispatched, grad_pre_all, preferred_element_type=f32
    )
    grad_down_full = jnp.einsum("ecf,ecd->efd", hidden_all, slot_grad, preferred_element_type=f32)
    grad_both, grad_down = (
        lax.psum_scatter(grad_both_full, "dp", scatter_dimension=0, tiled=True),
        lax.psum_scatter(grad_down_full, "dp", scatter_dimension=0, tiled=True),
    )
    grad_gate = grad_both[:, :, :hidden_width]
    grad_up = grad_both[:, :, hidden_width:]
    token_grad = jnp.sum(
        jnp.take(slot_input, slot_of, axis=0).reshape(length, TOPK, feature_part), axis=1
    )
    grad_normed_ffn = col_total(token_grad) + jnp.dot(
        grad_logits, w_router.T, preferred_element_type=f32
    )
    grad_ffn_in, grad_gain2 = norm_backward(resid_mid, scale_ffn, norm_gain2, grad_normed_ffn)
    grad_mid = grad_top + grad_ffn_in
    grad_mid_low = grad_mid.astype(low)
    grad_out_part = jnp.dot(attended_all.T, grad_mid_low, preferred_element_type=f32)
    grad_attended = head_share(jnp.dot(grad_mid_low, w_out.T, preferred_element_type=f32)).astype(
        low
    )
    grad_blocks = grad_attended.reshape(blocks, block_rows, heads_here, HEAD_DIM)

    def backward_block(carry, inputs):
        key_acc, value_acc = carry
        query_block, place_block, segment_block, attended_block, total_block, grad_block = inputs
        scores = block_scores(query_block, place_block, segment_block)
        weights = jnp.exp(scores - total_block)
        value_step = jnp.einsum(
            "hqk,qhd->khd", weights.astype(low), grad_block, preferred_element_type=f32
        )
        grad_weights = jnp.einsum(
            "qhd,khd->hqk", grad_block, values_wide, preferred_element_type=f32
        )
        delta_sum = jnp.sum(grad_block.astype(f32) * attended_block.astype(f32), axis=2).T[
            :, :, None
        ]
        grad_scores = (weights * (grad_weights - delta_sum)).astype(low)
        grad_query_block = (
            jnp.einsum("hqk,khd->qhd", grad_scores, keys_wide, preferred_element_type=f32)
            * score_scale
        )
        key_step = (
            jnp.einsum("hqk,qhd->khd", grad_scores, query_block, preferred_element_type=f32)
            * score_scale
        )
        return ((key_acc + key_step, value_acc + value_step), grad_query_block)

    zeros_wide = jnp.zeros((length, heads_here, HEAD_DIM), f32)
    (key_acc, value_acc), grad_query_blocks = lax.scan(
        backward_block,
        (zeros_wide, zeros_wide),
        (query_blocks, place_blocks, segment_blocks, attended_blocks, total_blocks, grad_blocks),
    )
    key_partial = jnp.sum(key_acc.reshape(length, key_heads, group_size, HEAD_DIM), axis=2).reshape(
        length, key_width
    )
    value_partial = jnp.sum(
        value_acc.reshape(length, key_heads, group_size, HEAD_DIM), axis=2
    ).reshape(length, key_width)
    key_value_grad = head_share(jnp.concatenate([key_partial, value_partial], axis=1))
    grad_queries = (
        rotate(grad_query_blocks.reshape(own_rows, heads_here, HEAD_DIM), cosine, -sine_part)
        .astype(low)
        .reshape(own_rows, query_width)
    )
    grad_keys = (
        rotate(
            key_value_grad[:, :key_width].reshape(own_rows, key_heads, HEAD_DIM), cosine, -sine_part
        )
        .astype(low)
        .reshape(own_rows, key_width)
    )
    grad_values = key_value_grad[:, key_width:].astype(low)
    grad_proj = head_collect(jnp.concatenate([grad_queries, grad_keys, grad_values], axis=1))
    grad_joined = jnp.dot(normed_attn.T, grad_proj, preferred_element_type=f32)
    grad_normed_attn = col_total(jnp.dot(grad_proj, joined_proj.T, preferred_element_type=f32))
    grad_attn_in, grad_gain1 = norm_backward(residual, scale_attn, norm_gain1, grad_normed_attn)
    grad_input = (grad_mid + grad_attn_in).astype(low)
    joined_sum, out_sum, router_sum, gain1_sum, gain2_sum = lax.psum(
        (grad_joined, grad_out_part, grad_router, grad_gain1, grad_gain2), "dp"
    )
    return (
        block_out,
        grad_input,
        joined_sum[:, :query_width],
        joined_sum[:, query_width : query_width + key_width],
        joined_sum[:, query_width + key_width :],
        out_sum,
        router_sum,
        grad_gate,
        grad_up,
        grad_down,
        gain1_sum,
        gain2_sum,
    )


def solution(mesh):
    placed = (
        P("dp", "row"),
        P("dp", None),
        P("dp", None),
        P("dp", "row"),
        P("row"),
        P("row", "col"),
        P("row", "col"),
        P("row", "col"),
        P("col", "row"),
        P("row"),
        P("row", None),
        P(None, "row", "col"),
        P(None, "row", "col"),
        P(None, "col", "row"),
    )
    return jax.shard_map(
        on_device,
        mesh=mesh,
        in_specs=placed,
        out_specs=(
            P("dp", "row"),
            P("dp", "row"),
            P("row", "col"),
            P("row", "col"),
            P("row", "col"),
            P("col", "row"),
            P("row", None),
            P("dp", "row", "col"),
            P("dp", "row", "col"),
            P("dp", "col", "row"),
            P("row"),
            P("row"),
        ),
        check_vma=False,
    )
```

profile of v0, /device:TPU:0, one launch (start us, length us, event | category | flops | bytes accessed | tf_op | source)
XLA Modules:
  0.0 1184.1 jit_solution(17169282977297748467)
XLA Ops:
  8.4 11.9 %psum.105 = f32[512]{0:T(512)S(1)} all-reduce(f32[512]{0:T(512)S(1)} %fusion.10), channel_id=1, replica_groups=mesh['dp'=16,'row'=4,'col'=2] {'row'}, use_global_device_ids=true, to_apply=%region_1.0 | all-reduce | flops 512 | bytes 4096 | tf_op jit(solution)/shard_map/psum | solution.py:51
  28.1 9.2 reduce-window.6
  38.9 15.5 %scatter_custom_fusion = s32[5120]{0:T(1024)S(1)} fusion(s32[4096]{0:T(1024)S(1)} %bitcast.134, s32[4096]{0:T(1024)S(1)} %iota.35, s32[]{:T(128)} %constant.152.clone.1), kind=kCustom, calls=%fused_computation.130 | custom fusion | bytes 20484 | tf_op jit(solution)/shard_map/scatter | solution.py:45
  59.8 13.5 %all_gather.15 = bf16[512,512]{1,0:T(8,128)(2,1)S(1)} all-gather(bf16[128,512]{1,0:T(8,128)(2,1)S(1)} %pad_maximum_fusion.3), channel_id=1, replica_groups=mesh['dp'=16,'row'=4,'col'=2] {'row'}, dimensions={0}, use_global_device_ids=true | all-gather | bytes 655360 | tf_op jit(solution)/shard_map/all_gather | solution.py:63
  76.6 13.0 %all_gather.16 = bf16[512,512]{0,1:T(8,128)(2,1)S(1)} all-gather(bf16[128,512]{0,1:T(8,128)(2,1)S(1)} %bitcast.123), channel_id=1, replica_groups=mesh['dp'=16,'row'=4,'col'=2] {'row'}, dimensions={0}, use_global_device_ids=true | all-gather | bytes 655360 | tf_op jit(solution)/shard_map/all_gather | solution.py:63
  101.2 26.6 %all-reduce.11.cloned.1.call-done = f32[512,256]{1,0:T(8,128)} async-done(((f32[512,256]{1,0:T(8,128)}), f32[512,256]{1,0:T(8,128)}) %all-reduce.11.cloned.1.call-update) | async-done | bytes 524304 | tf_op jit(solution)/shard_map/psum | solution.py:55
  129.0 10.7 psum.107
  140.5 18.2 %gather_fusion = bf16[5120,256]{1,0:T(8,128)(2,1)S(1)} fusion(bf16[513,256]{1,0:T(8,128)(2,1)S(1)} %concatenate.45, s32[5120]{0:T(1024)S(1)} %get-tuple-element.121), kind=kCustom, calls=%fused_computation.2 | custom fusion | bytes 5263360 | tf_op jit(solution)/shard_map/jit(_take)/gather | solution.py:184
  158.7 8.1 fusion.3
  168.4 95.0 %reduce-scatter.10.cloned.1.call-done = f32[1280,512]{1,0:T(8,128)} async-done(((f32[5120,512]{1,0:T(8,128)}), f32[1280,512]{1,0:T(8,128)}) %reduce-scatter.10.cloned.1.call-update) | async-done | bytes 2621456 | tf_op jit(solution)/shard_map/reduce_scatter | solution.py:67
  267.0 39.8 %all-reduce.13.cloned.1.call-done = f32[512,32]{0,1:T(8,128)} async-done(((f32[512,32]{0,1:T(8,128)}), f32[512,32]{0,1:T(8,128)}) %all-reduce.13.cloned.1.call-update) | async-done | bytes 65552 | tf_op jit(solution)/shard_map/psum | solution.py:179
  306.8 28.9 %gather_fusion.2 = f32[4096]{0:T(1024)S(1)} fusion(f32[512,32]{0,1:T(8,128)} %all-reduce.13.cloned.1.call-done, s32[4096]{0:T(1024)S(1)} %reshape.440), kind=kCustom, calls=%fused_computation.4 | custom fusion | bytes 65536 | tf_op jit(solution)/shard_map/jit(take_along_axis)/gather | solution.py:180
  336.0 8.1 all-gather.4.cloned.1.call-done
  350.3 18.7 %gather_fusion.3 = f32[4096,256]{1,0:T(8,128)} fusion(f32[5120,256]{1,0:T(8,128)} %bitcast.103, s32[4096]{0:T(1024)S(1)} %broadcast_clamp_fusion.1), kind=kCustom, calls=%fused_computation.clone | custom fusion | bytes 8404992 | tf_op jit(solution)/shard_map/jit(_take)/gather | solution.py:197
  372.1 32.4 %psum.111 = f32[512,8]{0,1:T(8,128)S(1)} all-reduce(f32[512,8]{0,1:T(8,128)S(1)} %copy.81), channel_id=1, replica_groups=mesh['dp'=16,'row'=4,'col'=2] {'row','col'}, use_global_device_ids=true, to_apply=%region_22.24 | all-reduce | flops 4096 | bytes 32768 | tf_op jit(solution)/shard_map/psum | solution.py:201
  406.7 21.0 %gather_fusion.1 = bf16[5120,256]{1,0:T(8,128)(2,1)} fusion(bf16[4097,256]{1,0:T(8,128)(2,1)S(1)} %concatenate.47, s32[5120]{0:T(1024)S(1)} %get-tuple-element.120), kind=kCustom, calls=%fused_computation.3 | custom fusion | bytes 5263360 | tf_op jit(solution)/shard_map/jit(_take)/gather | solution.py:210
  434.7 54.1 %reduce-scatter.12.cloned.1.call-done = f32[1280,256]{1,0:T(8,128)} async-done(((f32[5120,256]{1,0:T(8,128)}), f32[1280,256]{1,0:T(8,128)}) %reduce-scatter.12.cloned.1.call-update) | async-done | bytes 1310736 | tf_op jit(solution)/shard_map/reduce_scatter | solution.py:67
  492.0 56.9 %all-gather.6.cloned.1.call-done = bf16[5120,512]{1,0:T(8,128)(2,1)} async-done(((bf16[1280,512]{1,0:T(8,128)(2,1)}), bf16[5120,512]{1,0:T(8,128)(2,1)}) %all-gather.6.cloned.1.call-update) | async-done | bytes 5242896 | tf_op jit(solution)/shard_map/all_gather | solution.py:71
  548.9 10.1 fusion.64
  559.0 18.7 %gather_fusion.4 = f32[4096,256]{1,0:T(8,128)} fusion(f32[5120,256]{1,0:T(8,128)} %bitcast.102, s32[4096]{0:T(1024)S(1)} %broadcast_clamp_fusion.1), kind=kCustom, calls=%fused_computation.1.clone | custom fusion | bytes 8404992 | tf_op jit(solution)/shard_map/jit(_take)/gather | solution.py:238
  585.7 35.5 %all-reduce.15.cloned.1.call-done = f32[512,256]{1,0:T(8,128)} async-done(((f32[512,256]{1,0:T(8,128)}), f32[512,256]{1,0:T(8,128)}) %all-reduce.15.cloned.1.call-update) | async-done | bytes 524304 | tf_op jit(solution)/shard_map/psum | solution.py:55
  624.0 10.6 psum.112
  637.8 22.3 %reduce-scatter.14.cloned.1.call-done = f32[128,512]{1,0:T(8,128)} async-done(((f32[512,512]{1,0:T(8,128)}), f32[128,512]{1,0:T(8,128)}) %reduce-scatter.14.cloned.1.call-update) | async-done | bytes 262160 | tf_op jit(solution)/shard_map/reduce_scatter | solution.py:59
  669.3 22.4 %reduce-scatter.16.cloned.1.call-done = f32[128,512]{0,1:T(8,128)} async-done(((f32[512,512]{0,1:T(8,128)}), f32[128,512]{0,1:T(8,128)}) %reduce-scatter.16.cloned.1.call-update) | async-done | bytes 262160 | tf_op jit(solution)/shard_map/reduce_scatter | solution.py:59
  694.3 25.7 %all-gather.8.cloned.1.call-done = bf16[512,1024]{0,1:T(8,128)(2,1)} async-done(((bf16[128,1024]{0,1:T(8,128)(2,1)}), bf16[512,1024]{0,1:T(8,128)(2,1)}) %all-gather.8.cloned.1.call-update) | async-done | bytes 1048592 | tf_op jit(solution)/shard_map/all_gather | solution.py:63
  728.1 9.1 fusion.2
  745.7 25.5 %all-reduce.19.cloned.1.call-done = (f32[512,256]{1,0:T(8,128)}, f32[512,256]{1,0:T(8,128)}) async-done(((f32[512,256]{1,0:T(8,128)}, f32[512,256]{1,0:T(8,128)}), (f32[512,256]{1,0:T(8,128)}, f32[512,256]{1,0:T(8,128)})) %all-reduce.19.cloned.1.call-update) | async-done | bytes 1048592 | tf_op jit(solution)/shard_map/psum | solution.py:55
  772.5 10.7 psum.114
  783.2 67.6 %all-reduce.2 = (f32[256,32]{0,1:T(8,128)}, f32[256]{0:T(256)}, f32[256]{0:T(256)}) all-reduce(f32[256,32]{0,1:T(8,128)S(1)} %fusion.66, f32[256]{0:T(256)S(1)} %get-tuple-element.73, f32[256]{0:T(256)S(1)} %copy-done.50), channel_id=1, replica_groups=mesh['dp'=16,'row'=4,'col'=2] {'dp'}, use_global_device_ids=true, to_apply=%region_37.39 | all-reduce | flops 8704 | bytes 69632 | tf_op jit(solution)/shard_map/psum | solution.py:308
  854.7 63.4 %all-reduce.17.cloned.1.call-done = (f32[256,1024]{1,0:T(8,128)}, f32[512,256]{1,0:T(8,128)}) async-done(((f32[256,1024]{1,0:T(8,128)}, f32[512,256]{1,0:T(8,128)}), (f32[256,1024]{1,0:T(8,128)}, f32[512,256]{1,0:T(8,128)})) %all-reduce.17.cloned.1.call-update) | async-done | bytes 1572880 | tf_op jit(solution)/shard_map/psum | solution.py:308
  921.8 149.2 %reduce-scatter.18.cloned.1.call-done = f32[2,256,512]{2,1,0:T(8,128)} async-done(((f32[32,256,512]{2,1,0:T(8,128)}), f32[2,256,512]{2,1,0:T(8,128)}) %reduce-scatter.18.cloned.1.call-update) | async-done | bytes 1048592 | tf_op jit(solution)/shard_map/reduce_scatter | solution.py:232
  1073.3 103.5 %reduce-scatter.20.cloned.1.call-done = f32[2,256,256]{2,1,0:T(8,128)} async-done(((f32[32,256,256]{2,1,0:T(8,128)}), f32[2,256,256]{2,1,0:T(8,128)}) %reduce-scatter.20.cloned.1.call-update) | async-done | bytes 524304 | tf_op jit(solution)/shard_map/reduce_scatter | solution.py:233
  (248 shorter events, 113.4 us)
Async XLA Ops:
  7.2 83.3 %copy-start = (bf16[512,256]{1,0:T(8,128)(2,1)S(1)}, bf16[512,256]{1,0:T(8,128)(2,1)}, u32[]{:S(2)}) copy-start(bf16[512,256]{1,0:T(8,128)(2,1)} %param.24) | copy-start | bytes 786436
  7.2 49.3 %reduce-scatter.8.cloned.1.call-start = ((), (), s32[]{:S(2)}) async-start(), calls=%async_computation.7 | async-start | bytes 2621440 | tf_op jit(solution)/shard_map/reduce_scatter | solution.py:59
  27.2 100.6 %all-reduce.11.cloned.1.call-start = ((), (), s32[]{:S(2)}) async-start(), calls=%async_computation.8 | async-start | bytes 1048576 | tf_op jit(solution)/shard_map/psum | solution.py:55
  91.7 171.7 %reduce-scatter.10.cloned.1.call-start = ((), (), s32[]{:S(2)}) async-start(), calls=%async_computation.10 | async-start | bytes 13107200 | tf_op jit(solution)/shard_map/reduce_scatter | solution.py:67
  96.5 31.3 %copy-start.9 = (bf16[512,256]{1,0:T(8,128)(2,1)S(1)}, bf16[512,256]{1,0:T(8,128)(2,1)}, u32[]{:S(2)}) copy-start(bf16[512,256]{1,0:T(8,128)(2,1)} %param.16) | copy-start | bytes 786436
  96.5 43.8 %copy-start.45 = (f32[256]{0:T(256)S(1)}, f32[256]{0:T(256)}, u32[]{:S(2)}) copy-start(f32[256]{0:T(256)} %param.25) | copy-start | bytes 3076
  166.8 100.1 %copy-start.27 = (bf16[512,256]{1,0:T(8,128)(2,1)S(1)}, bf16[512,256]{1,0:T(8,128)(2,1)}, u32[]{:S(2)}) copy-start(bf16[512,256]{1,0:T(8,128)(2,1)} %param.19) | copy-start | bytes 786436
  166.8 140.0 %all-reduce.13.cloned.1.call-start = ((), (), s32[]{:S(2)}) async-start(), calls=%async_computation.9 | async-start | bytes 131072 | tf_op jit(solution)/shard_map/psum | solution.py:179
  168.3 175.8 %all-gather.4.cloned.1.call-start = ((), (), s32[]{:S(2)}) async-start(), calls=%async_computation.11 | async-start | bytes 3276800 | tf_op jit(solution)/shard_map/all_gather | solution.py:71
  266.3 222.5 %reduce-scatter.12.cloned.1.call-start = ((), (), s32[]{:S(2)}) async-start(), calls=%async_computation.12 | async-start | bytes 6553600 | tf_op jit(solution)/shard_map/reduce_scatter | solution.py:67
  434.6 54.2 %copy-start.8 = (f32[1280,512]{1,0:T(8,128)S(1)}, f32[1280,512]{1,0:T(8,128)}, u32[]{:S(2)}) copy-start(f32[1280,512]{1,0:T(8,128)} %reduce-scatter.10.cloned.1.call-done) | copy-start | bytes 7864324
  434.7 114.2 %all-gather.6.cloned.1.call-start = ((), (), s32[]{:S(2)}) async-start(), calls=%async_computation.13 | async-start | bytes 6553600 | tf_op jit(solution)/shard_map/all_gather | solution.py:71
  491.9 129.3 %all-reduce.15.cloned.1.call-start = ((), (), s32[]{:S(2)}) async-start(), calls=%async_computation.14 | async-start | bytes 1048576 | tf_op jit(solution)/shard_map/psum | solution.py:55
  577.7 43.5 %copy-start.7 = (f32[512,256]{1,0:T(8,128)S(1)}, f32[512,256]{1,0:T(8,128)}, u32[]{:S(2)}) copy-start(f32[512,256]{1,0:T(8,128)} %copy-done.6) | copy-start | bytes 1572868
  577.7 43.5 %copy-start.46 = (f32[256]{0:T(256)S(1)}, f32[256]{0:T(256)}, u32[]{:S(2)}) copy-start(f32[256]{0:T(256)} %param.25) | copy-start | bytes 3076
  577.7 56.9 %copy-start.49 = (f32[512]{0:T(512)S(1)}, f32[512]{0:T(512)}, u32[]{:S(2)}) copy-start(f32[512]{0:T(512)} %get-tuple-element.124) | copy-start | bytes 6148
  585.6 74.5 %reduce-scatter.14.cloned.1.call-start = ((), (), s32[]{:S(2)}) async-start(), calls=%async_computation.15 | async-start | bytes 1310720 | tf_op jit(solution)/shard_map/reduce_scatter | solution.py:59
  585.7 48.9 %copy-start.36 = (bf16[512,32]{0,1:T(8,128)(2,1)}, bf16[512,32]{0,1:T(8,128)(2,1)S(1)}, u32[]{:S(2)}) copy-start(bf16[512,32]{0,1:T(8,128)(2,1)S(1)} %select_reduce_fusion) | copy-start | bytes 98308
  634.6 29.2 %copy-start.2 = (f32[8,128,512]{2,1,0:T(8,128)S(1)}, f32[8,128,512]{2,1,0:T(8,128)}, u32[]{:S(2)}) copy-start(f32[8,128,512]{2,1,0:T(8,128)} %copy-done.1) | copy-start | bytes 6291460
  637.5 54.1 %reduce-scatter.16.cloned.1.call-start = ((), (), s32[]{:S(2)}) async-start(), calls=%async_computation.16 | async-start | bytes 1310720 | tf_op jit(solution)/shard_map/reduce_scatter | solution.py:59
  668.2 51.8 %copy-start.23 = (bf16[256,1024]{1,0:T(8,128)(2,1)S(1)}, bf16[256,1024]{1,0:T(8,128)(2,1)}, u32[]{:S(2)}) copy-start(bf16[256,1024]{1,0:T(8,128)(2,1)} %copy-done.22) | copy-start | bytes 1572868
  668.2 51.8 %all-gather.8.cloned.1.call-start = ((), (), s32[]{:S(2)}) async-start(), calls=%async_computation.17 | async-start | bytes 1310720 | tf_op jit(solution)/shard_map/all_gather | solution.py:63
  694.2 30.8 %copy-start.43 = (f32[512]{0:T(512)S(1)}, f32[512]{0:T(512)}, u32[]{:S(2)}) copy-start(f32[512]{0:T(512)} %copy-done.42) | copy-start | bytes 6148
  694.2 30.8 %copy-start.44 = (f32[256]{0:T(256)S(1)}, f32[256]{0:T(256)}, u32[]{:S(2)}) copy-start(f32[256]{0:T(256)} %param.20) | copy-start | bytes 3076
  694.3 76.9 %all-reduce.19.cloned.1.call-start = ((), (), s32[]{:S(2)}) async-start(), calls=%async_computation.21 | async-start | bytes 2097152 | tf_op jit(solution)/shard_map/psum | solution.py:55
  722.5 195.5 %all-reduce.17.cloned.1.call-start = ((), (), s32[]{:S(2)}) async-start(), calls=%async_computation.20 | async-start | bytes 3145728 | tf_op jit(solution)/shard_map/psum | solution.py:308
  728.0 343.0 %reduce-scatter.18.cloned.1.call-start = ((), (), s32[]{:S(2)}) async-start(), calls=%async_computation.18 | async-start | bytes 17825792 | tf_op jit(solution)/shard_map/reduce_scatter | solution.py:232
  737.1 439.7 %reduce-scatter.20.cloned.1.call-start = ((), (), s32[]{:S(2)}) async-start(), calls=%async_computation.19 | async-start | bytes 8912896 | tf_op jit(solution)/shard_map/reduce_scatter | solution.py:233
  744.6 38.6 %copy-start.50 = (f32[256]{0:T(256)S(1)}, f32[256]{0:T(256)}, u32[]{:S(2)}) copy-start(f32[256]{0:T(256)} %get-tuple-element.71) | copy-start | bytes 3076
  744.6 108.1 %copy-start.47 = (f32[512]{0:T(512)S(1)}, f32[512]{0:T(512)}, u32[]{:S(2)}) copy-start(f32[512]{0:T(512)} %get-tuple-element.122) | copy-start | bytes 6148
  745.5 107.1 %copy-start.14 = (f32[512,256]{1,0:T(8,128)S(1)}, f32[512,256]{1,0:T(8,128)}, u32[]{:S(2)}) copy-start(f32[512,256]{1,0:T(8,128)} %copy-done.13) | copy-start | bytes 1572868
  918.0 258.7 %copy-start.33 = (f32[512,256]{1,0:T(8,128)S(1)}, f32[512,256]{1,0:T(8,128)}, u32[]{:S(2)}) copy-start(f32[512,256]{1,0:T(8,128)} %get-tuple-element.139) | copy-start | bytes 1572868
  (35 other events, 263.0 us)
Sparse Core Ops, SparseCore 0:
  27.3 29.1 reduce-scatter.7
  91.8 35.9 all-reduce.10
  166.9 96.3 reduce-scatter.9
  266.1 40.6 all-reduce.12
  308.4 35.6 all-gather.3
  434.8 53.9 reduce-scatter.11
  492.1 56.7 all-gather.5
  585.7 35.5 all-reduce.14
  637.6 22.4 reduce-scatter.13
  668.3 23.2 reduce-scatter.15
  694.4 25.5 all-gather.7
  723.5 47.6 all-reduce.18
  774.5 143.4 all-reduce.16
  922.3 148.7 reduce-scatter.17
  1076.4 100.3 reduce-scatter.19
where the time goes:
time: 1190 us; the launch traced here: 1180 us
  waiting for transfers between devices  729 us (61%)
  blocking collectives  170 us (14%)
  local copies, waits for them, and re-layouts  157 us (13%)
  matrix products  66.7 us (6%)
  other arithmetic  44.7 us (4%)
  between operations  14.9 us (1%)
    reduce_scatter x1, waiting for transfers between devices, on_device(): lax.psum_scatter(grad_both_full, 'dp', scatter_dimension=0, tiled=True)  149 us
    reduce_scatter x2, waiting for transfers between devices, slot_share(): return lax.psum_scatter(matrix, 'row', scatter_dimension=0, tiled=True)  149 us
    reduce_scatter x1, waiting for transfers between devices, on_device(): lax.psum_scatter(grad_down_full, 'dp', scatter_dimension=0, tiled=True)  103 us
    psum x3, waiting for transfers between devices, col_total(): return lax.psum(matrix, 'col')  87.7 us
    psum x1, blocking collectives, on_device(): lax.psum((grad_joined, grad_out_part, grad_router, grad_gain1, grad_gain2...  67.6 us
    all_gather x2, waiting for transfers between devices, slot_collect(): return lax.all_gather(matrix, 'row', axis=0, tiled=True)  64.9 us
    psum x1, waiting for transfers between devices, on_device(): lax.psum((grad_joined, grad_out_part, grad_router, grad_gain1, grad_gain2...  63.4 us
    reduce_scatter x3, waiting for transfers between devices, head_share(): return lax.psum_scatter(matrix, 'row', scatter_dimension=0, tiled=True)  45.8 us
  transfers between devices with their start and end apart: 15, of which 15 were waited for; matrix products, arithmetic and copies ran while one was open for 9% of the time, Pallas kernels for 0%

commit v1 on v0

--- a/solution.py
+++ b/solution.py
@@ -198,7 +198,7 @@
     resid_out = resid_mid + col_total(jnp.sum(gate_probs[:, :, None] * picked, axis=1))
     block_out = resid_out.astype(low)
     grad_top = cotangent.astype(f32)
-    grad_prob = lax.psum(jnp.sum(grad_top[:, None, :] * picked, axis=2), ("row", "col"))
+    grad_prob = lax.psum(lax.psum(jnp.sum(grad_top[:, None, :] * picked, axis=2), "row"), "col")
     grad_chosen = gate_probs * (grad_prob - jnp.sum(gate_probs * grad_prob, axis=1, keepdims=True))
     expert_hits = (
         expert_ids[:, :, None] == jnp.arange(EXPERTS, dtype=jnp.int32)[None, None, :]

time: 1190 us -> 1180 us (level)
    psum x1 -> x2, blocking collectives: 32.4 us -> 23.1 us  [the longest x1 14.9 us: on_device(): lax.psum(jnp.sum(grad_top[:, None, :] * picked, axis=2), 'row')]
where the time goes in v1:
time: 1180 us; the launch traced here: 1170 us
  waiting for transfers between devices  730 us (62%)
  blocking collectives  161 us (14%)
  local copies, waits for them, and re-layouts  157 us (13%)
  matrix products  66.7 us (6%)
  other arithmetic  44.7 us (4%)
  between operations  14.9 us (1%)
    reduce_scatter x2, waiting for transfers between devices, slot_share(): return lax.psum_scatter(matrix, 'row', scatter_dimension=0, tiled=True)  149 us
    reduce_scatter x1, waiting for transfers between devices, on_device(): lax.psum_scatter(grad_both_full, 'dp', scatter_dimension=0, tiled=True)  149 us
    reduce_scatter x1, waiting for transfers between devices, on_device(): lax.psum_scatter(grad_down_full, 'dp', scatter_dimension=0, tiled=True)  103 us
    psum x3, waiting for transfers between devices, col_total(): return lax.psum(matrix, 'col')  87.6 us
    psum x1, blocking collectives, on_device(): lax.psum((grad_joined, grad_out_part, grad_router, grad_gain1, grad_gain2...  67.6 us
    all_gather x2, waiting for transfers between devices, slot_collect(): return lax.all_gather(matrix, 'row', axis=0, tiled=True)  64.9 us
    psum x1, waiting for transfers between devices, on_device(): lax.psum((grad_joined, grad_out_part, grad_router, grad_gain1, grad_gain2...  63.4 us
    reduce_scatter x3, waiting for transfers between devices, head_share(): return lax.psum_scatter(matrix, 'row', scatter_dimension=0, tiled=True)  45.8 us
  transfers between devices with their start and end apart: 15, of which 15 were waited for; matrix products, arithmetic and copies ran while one was open for 9% of the time, Pallas kernels for 0%

profile of v1, /device:TPU:0, one launch (start us, length us, event | category | flops | bytes accessed | tf_op | source)
XLA Modules:
  0.0 1174.9 jit_solution(314940548058402314)
XLA Ops:
  8.4 11.9 %psum.112 = f32[512]{0:T(512)S(1)} all-reduce(f32[512]{0:T(512)S(1)} %fusion.10), channel_id=1, replica_groups=mesh['dp'=16,'row'=4,'col'=2] {'row'}, use_global_device_ids=true, to_apply=%region_1.0 | all-reduce | flops 512 | bytes 4096 | tf_op jit(solution)/shard_map/psum | solution.py:51
  28.1 9.2 reduce-window.6
  38.9 15.5 %scatter_custom_fusion = s32[5120]{0:T(1024)S(1)} fusion(s32[4096]{0:T(1024)S(1)} %bitcast.134, s32[4096]{0:T(1024)S(1)} %iota.35, s32[]{:T(128)} %constant.152.clone.1), kind=kCustom, calls=%fused_computation.130 | custom fusion | bytes 20484 | tf_op jit(solution)/shard_map/scatter | solution.py:45
  59.9 13.5 %all_gather.15 = bf16[512,512]{1,0:T(8,128)(2,1)S(1)} all-gather(bf16[128,512]{1,0:T(8,128)(2,1)S(1)} %pad_maximum_fusion.3), channel_id=1, replica_groups=mesh['dp'=16,'row'=4,'col'=2] {'row'}, dimensions={0}, use_global_device_ids=true | all-gather | bytes 655360 | tf_op jit(solution)/shard_map/all_gather | solution.py:63
  76.7 13.0 %all_gather.16 = bf16[512,512]{0,1:T(8,128)(2,1)S(1)} all-gather(bf16[128,512]{0,1:T(8,128)(2,1)S(1)} %bitcast.123), channel_id=1, replica_groups=mesh['dp'=16,'row'=4,'col'=2] {'row'}, dimensions={0}, use_global_device_ids=true | all-gather | bytes 655360 | tf_op jit(solution)/shard_map/all_gather | solution.py:63
  101.2 26.6 %all-reduce.11.cloned.1.call-done = f32[512,256]{1,0:T(8,128)} async-done(((f32[512,256]{1,0:T(8,128)}), f32[512,256]{1,0:T(8,128)}) %all-reduce.11.cloned.1.call-update) | async-done | bytes 524304 | tf_op jit(solution)/shard_map/psum | solution.py:55
  129.0 10.7 psum.114
  140.5 18.2 %gather_fusion = bf16[5120,256]{1,0:T(8,128)(2,1)S(1)} fusion(bf16[513,256]{1,0:T(8,128)(2,1)S(1)} %concatenate.45, s32[5120]{0:T(1024)S(1)} %get-tuple-element.121), kind=kCustom, calls=%fused_computation.2 | custom fusion | bytes 5263360 | tf_op jit(solution)/shard_map/jit(_take)/gather | solution.py:184
  158.7 8.1 fusion.3
  168.4 95.0 %reduce-scatter.10.cloned.1.call-done = f32[1280,512]{1,0:T(8,128)} async-done(((f32[5120,512]{1,0:T(8,128)}), f32[1280,512]{1,0:T(8,128)}) %reduce-scatter.10.cloned.1.call-update) | async-done | bytes 2621456 | tf_op jit(solution)/shard_map/reduce_scatter | solution.py:67
  267.0 39.8 %all-reduce.13.cloned.1.call-done = f32[512,32]{0,1:T(8,128)} async-done(((f32[512,32]{0,1:T(8,128)}), f32[512,32]{0,1:T(8,128)}) %all-reduce.13.cloned.1.call-update) | async-done | bytes 65552 | tf_op jit(solution)/shard_map/psum | solution.py:179
  306.8 28.9 %gather_fusion.2 = f32[4096]{0:T(1024)S(1)} fusion(f32[512,32]{0,1:T(8,128)} %all-reduce.13.cloned.1.call-done, s32[4096]{0:T(1024)S(1)} %reshape.440), kind=kCustom, calls=%fused_computation.4 | custom fusion | bytes 65536 | tf_op jit(solution)/shard_map/jit(take_along_axis)/gather | solution.py:180
  350.3 18.6 %gather_fusion.3 = f32[4096,256]{1,0:T(8,128)} fusion(f32[5120,256]{1,0:T(8,128)} %bitcast.103, s32[4096]{0:T(1024)S(1)} %broadcast_clamp_fusion.1), kind=kCustom, calls=%fused_computation.clone | custom fusion | bytes 8404992 | tf_op jit(solution)/shard_map/jit(_take)/gather | solution.py:197
  372.0 14.9 %psum.118 = f32[512,8]{0,1:T(8,128)S(1)} all-reduce(f32[512,8]{0,1:T(8,128)S(1)} %copy.81), channel_id=1, replica_groups=mesh['dp'=16,'row'=4,'col'=2] {'row'}, use_global_device_ids=true, to_apply=%region_22.24 | all-reduce | flops 4096 | bytes 32768 | tf_op jit(solution)/shard_map/psum | solution.py:201
  386.9 8.1 psum.119
  397.3 20.9 %gather_fusion.1 = bf16[5120,256]{1,0:T(8,128)(2,1)} fusion(bf16[4097,256]{1,0:T(8,128)(2,1)S(1)} %concatenate.47, s32[5120]{0:T(1024)S(1)} %get-tuple-element.120), kind=kCustom, calls=%fused_computation.3 | custom fusion | bytes 5263360 | tf_op jit(solution)/shard_map/jit(_take)/gather | solution.py:210
  425.2 54.4 %reduce-scatter.12.cloned.1.call-done = f32[1280,256]{1,0:T(8,128)} async-done(((f32[5120,256]{1,0:T(8,128)}), f32[1280,256]{1,0:T(8,128)}) %reduce-scatter.12.cloned.1.call-update) | async-done | bytes 1310736 | tf_op jit(solution)/shard_map/reduce_scatter | solution.py:67
  482.8 56.9 %all-gather.6.cloned.1.call-done = bf16[5120,512]{1,0:T(8,128)(2,1)} async-done(((bf16[1280,512]{1,0:T(8,128)(2,1)}), bf16[5120,512]{1,0:T(8,128)(2,1)}) %all-gather.6.cloned.1.call-update) | async-done | bytes 5242896 | tf_op jit(solution)/shard_map/all_gather | solution.py:71
  539.7 10.1 fusion.64
  549.8 18.6 %gather_fusion.4 = f32[4096,256]{1,0:T(8,128)} fusion(f32[5120,256]{1,0:T(8,128)} %bitcast.102, s32[4096]{0:T(1024)S(1)} %broadcast_clamp_fusion.1), kind=kCustom, calls=%fused_computation.1.clone | custom fusion | bytes 8404992 | tf_op jit(solution)/shard_map/jit(_take)/gather | solution.py:238
  576.4 35.5 %all-reduce.15.cloned.1.call-done = f32[512,256]{1,0:T(8,128)} async-done(((f32[512,256]{1,0:T(8,128)}), f32[512,256]{1,0:T(8,128)}) %all-reduce.15.cloned.1.call-update) | async-done | bytes 524304 | tf_op jit(solution)/shard_map/psum | solution.py:55
  614.7 10.6 psum.120
  628.5 22.2 %reduce-scatter.14.cloned.1.call-done = f32[128,512]{1,0:T(8,128)} async-done(((f32[512,512]{1,0:T(8,128)}), f32[128,512]{1,0:T(8,128)}) %reduce-scatter.14.cloned.1.call-update) | async-done | bytes 262160 | tf_op jit(solution)/shard_map/reduce_scatter | solution.py:59
  659.9 22.5 %reduce-scatter.16.cloned.1.call-done = f32[128,512]{0,1:T(8,128)} async-done(((f32[512,512]{0,1:T(8,128)}), f32[128,512]{0,1:T(8,128)}) %reduce-scatter.16.cloned.1.call-update) | async-done | bytes 262160 | tf_op jit(solution)/shard_map/reduce_scatter | solution.py:59
  685.0 25.7 %all-gather.8.cloned.1.call-done = bf16[512,1024]{0,1:T(8,128)(2,1)} async-done(((bf16[128,1024]{0,1:T(8,128)(2,1)}), bf16[512,1024]{0,1:T(8,128)(2,1)}) %all-gather.8.cloned.1.call-update) | async-done | bytes 1048592 | tf_op jit(solution)/shard_map/all_gather | solution.py:63
  718.8 9.1 fusion.2
  736.4 25.5 %all-reduce.19.cloned.1.call-done = (f32[512,256]{1,0:T(8,128)}, f32[512,256]{1,0:T(8,128)}) async-done(((f32[512,256]{1,0:T(8,128)}, f32[512,256]{1,0:T(8,128)}), (f32[512,256]{1,0:T(8,128)}, f32[512,256]{1,0:T(8,128)})) %all-reduce.19.cloned.1.call-update) | async-done | bytes 1048592 | tf_op jit(solution)/shard_map/psum | solution.py:55
  763.3 10.7 psum.122
  773.9 67.6 %all-reduce.2 = (f32[256,32]{0,1:T(8,128)}, f32[256]{0:T(256)}, f32[256]{0:T(256)}) all-reduce(f32[256,32]{0,1:T(8,128)S(1)} %fusion.66, f32[256]{0:T(256)S(1)} %get-tuple-element.73, f32[256]{0:T(256)S(1)} %copy-done.50), channel_id=1, replica_groups=mesh['dp'=16,'row'=4,'col'=2] {'dp'}, use_global_device_ids=true, to_apply=%region_38.40 | all-reduce | flops 8704 | bytes 69632 | tf_op jit(solution)/shard_map/psum | solution.py:308
  845.4 63.4 %all-reduce.17.cloned.1.call-done = (f32[256,1024]{1,0:T(8,128)}, f32[512,256]{1,0:T(8,128)}) async-done(((f32[256,1024]{1,0:T(8,128)}, f32[512,256]{1,0:T(8,128)}), (f32[256,1024]{1,0:T(8,128)}, f32[512,256]{1,0:T(8,128)})) %all-reduce.17.cloned.1.call-update) | async-done | bytes 1572880 | tf_op jit(solution)/shard_map/psum | solution.py:308
  912.6 149.2 %reduce-scatter.18.cloned.1.call-done = f32[2,256,512]{2,1,0:T(8,128)} async-done(((f32[32,256,512]{2,1,0:T(8,128)}), f32[2,256,512]{2,1,0:T(8,128)}) %reduce-scatter.18.cloned.1.call-update) | async-done | bytes 1048592 | tf_op jit(solution)/shard_map/reduce_scatter | solution.py:232
  1064.0 103.5 %reduce-scatter.20.cloned.1.call-done = f32[2,256,256]{2,1,0:T(8,128)} async-done(((f32[32,256,256]{2,1,0:T(8,128)}), f32[2,256,256]{2,1,0:T(8,128)}) %reduce-scatter.20.cloned.1.call-update) | async-done | bytes 524304 | tf_op jit(solution)/shard_map/reduce_scatter | solution.py:233
  (249 shorter events, 121.5 us)
Async XLA Ops:
  7.2 83.3 %copy-start = (bf16[512,256]{1,0:T(8,128)(2,1)S(1)}, bf16[512,256]{1,0:T(8,128)(2,1)}, u32[]{:S(2)}) copy-start(bf16[512,256]{1,0:T(8,128)(2,1)} %param.24) | copy-start | bytes 786436
  7.2 49.4 %reduce-scatter.8.cloned.1.call-start = ((), (), s32[]{:S(2)}) async-start(), calls=%async_computation.7 | async-start | bytes 2621440 | tf_op jit(solution)/shard_map/reduce_scatter | solution.py:59
  27.2 100.6 %all-reduce.11.cloned.1.call-start = ((), (), s32[]{:S(2)}) async-start(), calls=%async_computation.8 | async-start | bytes 1048576 | tf_op jit(solution)/shard_map/psum | solution.py:55
  91.7 171.7 %reduce-scatter.10.cloned.1.call-start = ((), (), s32[]{:S(2)}) async-start(), calls=%async_computation.10 | async-start | bytes 13107200 | tf_op jit(solution)/shard_map/reduce_scatter | solution.py:67
  96.5 31.3 %copy-start.9 = (bf16[512,256]{1,0:T(8,128)(2,1)S(1)}, bf16[512,256]{1,0:T(8,128)(2,1)}, u32[]{:S(2)}) copy-start(bf16[512,256]{1,0:T(8,128)(2,1)} %param.16) | copy-start | bytes 786436
  96.5 43.8 %copy-start.45 = (f32[256]{0:T(256)S(1)}, f32[256]{0:T(256)}, u32[]{:S(2)}) copy-start(f32[256]{0:T(256)} %param.25) | copy-start | bytes 3076
  166.8 100.1 %copy-start.27 = (bf16[512,256]{1,0:T(8,128)(2,1)S(1)}, bf16[512,256]{1,0:T(8,128)(2,1)}, u32[]{:S(2)}) copy-start(bf16[512,256]{1,0:T(8,128)(2,1)} %param.19) | copy-start | bytes 786436
  166.8 140.0 %all-reduce.13.cloned.1.call-start = ((), (), s32[]{:S(2)}) async-start(), calls=%async_computation.9 | async-start | bytes 131072 | tf_op jit(solution)/shard_map/psum | solution.py:179
  168.3 175.8 %all-gather.4.cloned.1.call-start = ((), (), s32[]{:S(2)}) async-start(), calls=%async_computation.11 | async-start | bytes 3276800 | tf_op jit(solution)/shard_map/all_gather | solution.py:71
  266.3 213.3 %reduce-scatter.12.cloned.1.call-start = ((), (), s32[]{:S(2)}) async-start(), calls=%async_computation.12 | async-start | bytes 6553600 | tf_op jit(solution)/shard_map/reduce_scatter | solution.py:67
  425.2 54.5 %copy-start.8 = (f32[1280,512]{1,0:T(8,128)S(1)}, f32[1280,512]{1,0:T(8,128)}, u32[]{:S(2)}) copy-start(f32[1280,512]{1,0:T(8,128)} %reduce-scatter.10.cloned.1.call-done) | copy-start | bytes 7864324
  425.2 114.5 %all-gather.6.cloned.1.call-start = ((), (), s32[]{:S(2)}) async-start(), calls=%async_computation.13 | async-start | bytes 6553600 | tf_op jit(solution)/shard_map/all_gather | solution.py:71
  482.7 129.2 %all-reduce.15.cloned.1.call-start = ((), (), s32[]{:S(2)}) async-start(), calls=%async_computation.14 | async-start | bytes 1048576 | tf_op jit(solution)/shard_map/psum | solution.py:55
  568.4 43.5 %copy-start.7 = (f32[512,256]{1,0:T(8,128)S(1)}, f32[512,256]{1,0:T(8,128)}, u32[]{:S(2)}) copy-start(f32[512,256]{1,0:T(8,128)} %copy-done.6) | copy-start | bytes 1572868
  568.4 43.5 %copy-start.46 = (f32[256]{0:T(256)S(1)}, f32[256]{0:T(256)}, u32[]{:S(2)}) copy-start(f32[256]{0:T(256)} %param.25) | copy-start | bytes 3076
  568.4 56.9 %copy-start.49 = (f32[512]{0:T(512)S(1)}, f32[512]{0:T(512)}, u32[]{:S(2)}) copy-start(f32[512]{0:T(512)} %get-tuple-element.124) | copy-start | bytes 6148
  576.3 74.5 %reduce-scatter.14.cloned.1.call-start = ((), (), s32[]{:S(2)}) async-start(), calls=%async_computation.15 | async-start | bytes 1310720 | tf_op jit(solution)/shard_map/reduce_scatter | solution.py:59
  576.4 48.9 %copy-start.36 = (bf16[512,32]{0,1:T(8,128)(2,1)}, bf16[512,32]{0,1:T(8,128)(2,1)S(1)}, u32[]{:S(2)}) copy-start(bf16[512,32]{0,1:T(8,128)(2,1)S(1)} %select_reduce_fusion) | copy-start | bytes 98308
  625.3 29.1 %copy-start.2 = (f32[8,128,512]{2,1,0:T(8,128)S(1)}, f32[8,128,512]{2,1,0:T(8,128)}, u32[]{:S(2)}) copy-start(f32[8,128,512]{2,1,0:T(8,128)} %copy-done.1) | copy-start | bytes 6291460
  628.2 54.2 %reduce-scatter.16.cloned.1.call-start = ((), (), s32[]{:S(2)}) async-start(), calls=%async_computation.16 | async-start | bytes 1310720 | tf_op jit(solution)/shard_map/reduce_scatter | solution.py:59
  658.8 52.0 %copy-start.23 = (bf16[256,1024]{1,0:T(8,128)(2,1)S(1)}, bf16[256,1024]{1,0:T(8,128)(2,1)}, u32[]{:S(2)}) copy-start(bf16[256,1024]{1,0:T(8,128)(2,1)} %copy-done.22) | copy-start | bytes 1572868
  658.8 51.9 %all-gather.8.cloned.1.call-start = ((), (), s32[]{:S(2)}) async-start(), calls=%async_computation.17 | async-start | bytes 1310720 | tf_op jit(solution)/shard_map/all_gather | solution.py:63
  685.0 30.8 %copy-start.43 = (f32[512]{0:T(512)S(1)}, f32[512]{0:T(512)}, u32[]{:S(2)}) copy-start(f32[512]{0:T(512)} %copy-done.42) | copy-start | bytes 6148
  685.0 30.8 %copy-start.44 = (f32[256]{0:T(256)S(1)}, f32[256]{0:T(256)}, u32[]{:S(2)}) copy-start(f32[256]{0:T(256)} %param.20) | copy-start | bytes 3076
  685.0 76.9 %all-reduce.19.cloned.1.call-start = ((), (), s32[]{:S(2)}) async-start(), calls=%async_computation.21 | async-start | bytes 2097152 | tf_op jit(solution)/shard_map/psum | solution.py:55
  713.3 195.5 %all-reduce.17.cloned.1.call-start = ((), (), s32[]{:S(2)}) async-start(), calls=%async_computation.20 | async-start | bytes 3145728 | tf_op jit(solution)/shard_map/psum | solution.py:308
  718.7 343.0 %reduce-scatter.18.cloned.1.call-start = ((), (), s32[]{:S(2)}) async-start(), calls=%async_computation.18 | async-start | bytes 17825792 | tf_op jit(solution)/shard_map/reduce_scatter | solution.py:232
  727.9 439.6 %reduce-scatter.20.cloned.1.call-start = ((), (), s32[]{:S(2)}) async-start(), calls=%async_computation.19 | async-start | bytes 8912896 | tf_op jit(solution)/shard_map/reduce_scatter | solution.py:233
  735.3 38.6 %copy-start.50 = (f32[256]{0:T(256)S(1)}, f32[256]{0:T(256)}, u32[]{:S(2)}) copy-start(f32[256]{0:T(256)} %get-tuple-element.71) | copy-start | bytes 3076
  735.3 108.1 %copy-start.47 = (f32[512]{0:T(512)S(1)}, f32[512]{0:T(512)}, u32[]{:S(2)}) copy-start(f32[512]{0:T(512)} %get-tuple-element.122) | copy-start | bytes 6148
  736.3 107.1 %copy-start.14 = (f32[512,256]{1,0:T(8,128)S(1)}, f32[512,256]{1,0:T(8,128)}, u32[]{:S(2)}) copy-start(f32[512,256]{1,0:T(8,128)} %copy-done.13) | copy-start | bytes 1572868
  908.8 258.7 %copy-start.33 = (f32[512,256]{1,0:T(8,128)S(1)}, f32[512,256]{1,0:T(8,128)}, u32[]{:S(2)}) copy-start(f32[512,256]{1,0:T(8,128)} %get-tuple-element.139) | copy-start | bytes 1572868
  (35 other events, 262.9 us)
Sparse Core Ops, SparseCore 0:
  27.3 29.1 reduce-scatter.7
  91.8 35.9 all-reduce.10
  166.9 96.3 reduce-scatter.9
  266.1 40.6 all-reduce.12
  308.4 35.6 all-gather.3
  425.3 54.2 reduce-scatter.11
  482.8 56.7 all-gather.5
  576.4 35.5 all-reduce.14
  628.3 22.3 reduce-scatter.13
  658.9 23.4 reduce-scatter.15
  685.1 25.5 all-gather.7
  714.2 47.6 all-reduce.18
  765.3 143.4 all-reduce.16
  913.0 148.7 reduce-scatter.17
  1067.2 100.3 reduce-scatter.19
